TPU v7x, 32 devices: a whole 2x2x4 slice. The times are simulated.
32 devices in a mesh: layer: 8 (over z, x), shard: 4 (over y, core).
Axes of the slice: x: 2, y: 2, z: 4, core: 2. Of those that a mesh axis runs over, the one named last changes fastest.
Arguments:
- gate_grad: bfloat16 [8, 2048, 512], P('layer', 'shard'), parts along dimension 0, may hold values from -400 to 400
- gate_moment: bfloat16 [8, 2048, 512], P('layer', 'shard'), parts along dimension 0, may hold values from -120 to 120
- down_grad: bfloat16 [8, 2048, 512], P('layer', 'shard'), parts along dimension 0, may hold values from -400 to 400
- down_moment: bfloat16 [8, 2048, 512], P('layer', 'shard'), parts along dimension 0, may hold values from -120 to 120
Outputs:
- gate_update: bfloat16 [8, 2048, 512], P('layer', 'shard'), parts along dimension 0
- down_update: bfloat16 [8, 2048, 512], P('layer', 'shard'), parts along dimension 0
There are 8 independent parts, one for each index of `layer`. A program takes and returns all parts, laid end to end along the dimension named above; each array names one. Nothing has to cross between parts.
All inputs are finite; a program needn't handle non-finite values.
Results may differ from a plain program's by a relative error of at most 0.0068.
Values may be sent and summed in bfloat16 or wider, within the bound.
A program may use at most 64 MiB of HBM per device.

v0:
```python
import math

import jax
import jax.numpy as jnp
from jax import lax
from jax.sharding import PartitionSpec as P

D = 2048


MOMENTUM_RATE = 0.95
COEF_A = 3.4445
COEF_B = -4.775
COEF_C = 2.0315
EPSILON = 1e-07


def partner(block, axis, stride):
    count = lax.axis_size(axis)
    route = []
    for low in range(count):
        high = low | 1 << stride
        if high != low and high < count:
            route += [(low, high), (high, low)]
    return lax.ppermute(block, axis, route)


def blended(gradient, moment):
    buffer = MOMENTUM_RATE * moment.astype(jnp.float32) + gradient.astype(jnp.float32)
    return (gradient.astype(jnp.float32) + MOMENTUM_RATE * buffer).astype(jnp.bfloat16)


def transposed_product(first_matrix, second_matrix):
    return lax.dot_general(
        first_matrix, second_matrix, (((0,), (0,)), ((), ())), preferred_element_type=jnp.float32
    )


def quintic(current):
    square = jnp.dot(current, current, preferred_element_type=jnp.float32)
    identity = jnp.eye(current.shape[0], dtype=jnp.float32)
    return (COEF_A * identity + COEF_B * current.astype(jnp.float32) + COEF_C * square).astype(
        jnp.bfloat16
    )


def bit_value(position):
    return lax.axis_index("shard") // (1 << position) % 2


def ordered_total(ordered):
    total = ordered[0].astype(jnp.float32)
    for member in ordered[1:]:
        total = total + member.astype(jnp.float32)
    return total


def polish(owned_rows, total):
    factor = 1.0 / (jnp.sqrt(jnp.trace(total)) + EPSILON)
    scaled = (total * (factor * factor)).astype(jnp.bfloat16)
    combined = quintic(scaled)
    product = jnp.dot(scaled, combined, preferred_element_type=jnp.float32).astype(jnp.bfloat16)
    current = transposed_product(combined, product).astype(jnp.bfloat16)
    combined = jnp.dot(combined, quintic(current), preferred_element_type=jnp.float32).astype(
        jnp.bfloat16
    )
    result = jnp.dot(owned_rows, combined, preferred_element_type=jnp.float32) * (
        math.sqrt(D) * factor
    )
    return result.astype(jnp.bfloat16)


def paired_owners(gate_input, down_input, pair_bit):
    experts, row_count, columns = gate_input.shape
    matrices = 2 * experts
    group = 1 << pair_bit
    stacked = jnp.concatenate((gate_input, down_input), 0)
    outgoing = stacked.reshape(matrices // group, group, 2, row_count // 2, columns)
    outgoing = outgoing.transpose(0, 2, 1, 3, 4).reshape(matrices * 2, row_count // 2, columns)
    owned_rows = lax.all_to_all(outgoing, "shard", split_axis=0, concat_axis=1, tiled=True)[0]
    pieces = owned_rows.reshape(-1, 2, row_count // 4, columns)
    lower_rows = pieces[:, 0].reshape(-1, columns)
    upper_rows = pieces[:, 1].reshape(-1, columns)
    own_lower, own_upper = lax.optimization_barrier(
        (
            transposed_product(lower_rows, lower_rows).astype(jnp.bfloat16),
            transposed_product(upper_rows, upper_rows).astype(jnp.bfloat16),
        )
    )
    far_lower, far_upper = partner((own_lower, own_upper), "shard", pair_bit)
    high = bit_value(pair_bit) == 1
    ordered = (
        jnp.where(high, far_lower, own_lower),
        jnp.where(high, far_upper, own_upper),
        jnp.where(high, own_lower, far_lower),
        jnp.where(high, own_upper, far_upper),
    )
    result = polish(owned_rows, ordered_total(ordered))
    returned = lax.all_to_all(result[None], "shard", split_axis=1, concat_axis=0, tiled=True)
    restored = returned.reshape(matrices // group, 2, group, row_count // 2, columns)
    restored = restored.transpose(0, 2, 1, 3, 4).reshape(matrices, row_count, columns)
    return (restored[:experts], restored[experts:])


def shards(gate_grad, gate_moment, down_grad, down_moment):
    first_bit = 0
    gate_input = blended(gate_grad, gate_moment)
    down_input = blended(down_grad, down_moment)
    gate_update, down_update = paired_owners(gate_input, down_input, first_bit)
    return (gate_update, down_update)


def solution(mesh):
    in_specs = (
        P("layer", "shard", None),
        P("layer", "shard", None),
        P("layer", "shard", None),
        P("layer", "shard", None),
    )
    out_specs = (P("layer", "shard", None), P("layer", "shard", None))
    return jax.shard_map(shards, mesh=mesh, in_specs=in_specs, out_specs=out_specs, check_vma=False)
```

profile of v0, /device:TPU:0, one launch (start us, length us, event | category | flops | bytes accessed | tf_op | source)
XLA Modules:
  0.0 64.0 jit_solution(12169596544686060276)
XLA Ops:
  0.6 2.0 %fusion.8 = (bf16[1,512,512]{2,1,0:T(8,128)(2,1)S(1)}, bf16[1,512,512]{2,1,0:T(8,128)(2,1)S(1)}) fusion(bf16[1,512,512]{2,1,0:T(8,128)(2,1)} %param.4, bf16[1,512,512]{2,1,0:T(8,128)(2,1)} %param.5, bf16[1,512,512]{2,1,0:T(8,128)(2,1)} %param.7, bf16[1,512,512]{2,1,0:T(8,128)(2,1)} %param.6), kind=kLoop, calls=%fused_computation.22 | loop fusion | flops 3670016 | bytes 3145728 | tf_op jit(solution)/shard_map/convert_element_type | solution.py:30
  2.6 0.1 pad_maximum_fusion
  2.7 18.5 %all_to_all.21 = bf16[4,256,512]{2,1,0:T(8,128)(2,1)S(1)} all-to-all(bf16[4,256,512]{2,1,0:T(8,128)(2,1)S(1)} %bitcast.39), channel_id=1, replica_groups=mesh['layer'=8,'shard'=4] {'shard'}, dimensions={0} | all-to-all | bytes 2097152 | tf_op jit(solution)/shard_map/all_to_all | solution.py:80
  21.2 0.5 fusion.5
  21.7 0.5 fusion.6
  22.2 0.1 collective-permute-start
  22.2 0.5 collective-permute-start.1
  22.7 1.4 %collective-permute-done = bf16[512,512]{1,0:T(8,128)(2,1)S(1)} collective-permute-done((bf16[512,512]{1,0:T(8,128)(2,1)S(1)}, bf16[512,512]{1,0:T(8,128)(2,1)S(1)}, u32[]{:S(2)}, u32[]{:S(2)}) %collective-permute-start) | collective-permute-done | bytes 524320 | tf_op jit(solution)/shard_map/ppermute | solution.py:25
  24.1 0.0 copy-start
  24.1 0.8 %copy-done = bf16[512,512]{1,0:T(8,128)(2,1)} copy-done((bf16[512,512]{1,0:T(8,128)(2,1)}, bf16[512,512]{1,0:T(8,128)(2,1)S(1)}, u32[]{:S(2)}) %copy-start) | copy-done | bytes 524312
  24.9 0.1 collective-permute-done.1
  25.0 2.2 %select_reduce_fusion = (f32[]{:T(128)}, f32[512,512]{1,0:T(8,128)S(1)}) fusion(bf16[512,512]{1,0:T(8,128)(2,1)S(1)} %fusion.6, bf16[512,512]{1,0:T(8,128)(2,1)} %collective-permute-done.1, bf16[512,512]{1,0:T(8,128)(2,1)S(1)} %fusion.5, bf16[512,512]{1,0:T(8,128)(2,1)} %copy-done, pred[]{:T(512)S(6)} %eq.16), kind=kLoop, calls=%fused_computation.29 | loop fusion | flops 3670015 | bytes 3145733 | tf_op jit(solution)/shard_map/jit(trace)/reduce_sum | solution.py:59
  28.0 0.5 fusion.3
  28.4 1.6 %convolution_convert_fusion.1 = bf16[512,512]{1,0:T(8,128)(2,1)} fusion(bf16[512,512]{1,0:T(8,128)(2,1)S(1)} %fusion.3, f32[512,512]{1,0:T(8,128)S(1)} %get-tuple-element.11, f32[]{:T(128)S(6)} %mul.50), kind=kOutput, calls=%fused_computation.17 | convolution fusion | flops 537919488 | bytes 2097156 | tf_op jit(solution)/shard_map/dot_general | solution.py:34
  30.0 2.3 %convolution_convert_fusion = bf16[512,512]{1,0:T(8,128)(2,1)S(1)} fusion(bf16[512,512]{1,0:T(8,128)(2,1)S(1)} %fusion.3, bf16[512,512]{1,0:T(8,128)(2,1)} %convolution_convert_fusion.1), kind=kOutput, calls=%fused_computation.16 | convolution fusion | flops 539230208 | bytes 1572864 | tf_op jit(solution)/shard_map/dot_general | solution.py:64
  32.3 0.7 %fusion = bf16[1,1024,512]{2,1,0:T(8,128)(2,1)S(1)} fusion(bf16[1024,512]{1,0:T(8,128)(2,1)S(1)} %bitcast.43, bf16[512,512]{1,0:T(8,128)(2,1)S(1)} %convolution_convert_fusion, f32[]{:T(128)S(6)} %mul_shard_map.3), kind=kOutput, calls=%fused_computation.3 | convolution fusion | flops 537919488 | bytes 2621444 | tf_op jit(solution)/shard_map/dot_general | solution.py:67
  33.0 1.6 %copy.30 = bf16[1,1024,512]{2,0,1:T(2,128)(2,1)S(1)} copy(bf16[1,1024,512]{2,1,0:T(8,128)(2,1)S(1)} %fusion) | data formatting | bytes 2097152 | tf_op jit(solution)/shard_map/broadcast_in_dim | solution.py:99
  34.7 0.5 broadcast.45
  35.2 7.0 %reduce = bf16[1024,512]{1,0:T(8,128)(2,1)S(1)} reduce(bf16[1024,1,512]{2,1,0:T(2,128)(2,1)S(1)} %bitcast.38, bf16[]{:T(256)} %broadcast.45), dimensions={1}, to_apply=%bitcast.35.reduce_sub_computation | reduce | bytes 2097154
  42.2 0.8 %reshape.28 = bf16[4,2,65536]{2,1,0:T(2,128)(2,1)S(1)} reshape(bf16[1024,512]{1,0:T(8,128)(2,1)S(1)} %reduce) | data formatting | bytes 2097152
  43.0 16.9 %all_to_all.22 = bf16[4,2,65536]{2,1,0:T(2,128)(2,1)S(1)} all-to-all(bf16[4,2,65536]{2,1,0:T(2,128)(2,1)S(1)} %reshape.28), channel_id=1, replica_groups=mesh['layer'=8,'shard'=4] {'shard'}, dimensions={0} | all-to-all | bytes 2097152 | tf_op jit(solution)/shard_map/all_to_all | solution.py:99
  59.9 0.9 %reshape.29 = bf16[1024,1,512]{2,1,0:T(2,128)(2,1)S(1)} reshape(bf16[4,2,65536]{2,1,0:T(2,128)(2,1)S(1)} %all_to_all.22) | data formatting | bytes 2097152
  60.9 0.3 copy.26
  61.1 1.1 %slice.24 = bf16[1,512,512]{2,0,1:T(2,128)(2,1)S(1)} slice(bf16[1,1024,512]{2,0,1:T(2,128)(2,1)S(1)} %bitcast.37), slice={[0:1], [512:1024], [0:512]} | slice | bytes 1048576 | tf_op jit(solution)/shard_map/slice | solution.py:102
  62.2 0.8 %slice.23 = bf16[1,2,256,512]{3,2,1,0:T(8,128)(2,1)} slice(bf16[1,4,256,512]{3,2,1,0:T(8,128)(2,1)S(1)} %bitcast.40), slice={[0:1], [0:2], [0:256], [0:512]} | slice | bytes 1048576 | tf_op jit(solution)/shard_map/slice | solution.py:102
  63.1 0.9 %copy.23 = bf16[1,512,512]{2,1,0:T(8,128)(2,1)} copy(bf16[1,512,512]{2,0,1:T(2,128)(2,1)S(1)} %slice.24) | data formatting | bytes 1048576
Async XLA Ops:
  22.2 2.0 %collective-permute-start = (bf16[512,512]{1,0:T(8,128)(2,1)S(1)}, bf16[512,512]{1,0:T(8,128)(2,1)S(1)}, u32[]{:S(2)}, u32[]{:S(2)}) collective-permute-start(bf16[512,512]{1,0:T(8,128)(2,1)S(1)} %fusion.5), channel_id=1, source_target_pairs={{0,1},{1,0},{2,3},{3,2},{4,5},{5,4},{6,7},{7,6},{8,9},{9,8},{10,11... | collective-permute-start | bytes 1572872 | tf_op jit(solution)/shard_map/ppermute | solution.py:25
  22.2 2.8 %collective-permute-start.1 = (bf16[512,512]{1,0:T(8,128)(2,1)S(1)}, bf16[512,512]{1,0:T(8,128)(2,1)}, u32[]{:S(2)}, u32[]{:S(2)}) collective-permute-start(bf16[512,512]{1,0:T(8,128)(2,1)S(1)} %fusion.6), channel_id=1, source_target_pairs={{0,1},{1,0},{2,3},{3,2},{4,5},{5,4},{6,7},{7,6},{8,9},{9,8},{10,11... | collective-permute-start | bytes 1572872 | tf_op jit(solution)/shard_map/ppermute | solution.py:25
  24.1 0.8 %copy-start = (bf16[512,512]{1,0:T(8,128)(2,1)}, bf16[512,512]{1,0:T(8,128)(2,1)S(1)}, u32[]{:S(2)}) copy-start(bf16[512,512]{1,0:T(8,128)(2,1)S(1)} %collective-permute-done) | copy-start | bytes 1572868
where the time goes:
time: 64.3 us; the launch traced here: 64 us
  blocking collectives  35.4 us (55%)
  other arithmetic  11.3 us (18%)
  local copies, waits for them, and re-layouts  7.78 us (12%)
  matrix products  5.99 us (9%)
  waiting for transfers between devices  1.49 us (2%)
  between operations  1.47 us (2%)
    all_to_all x1, blocking collectives, paired_owners(): lax.all_to_all(outgoing, 'shard', split_axis=0, concat_axis=1, tiled=True)  18.5 us
    all_to_all x1, blocking collectives, paired_owners(): lax.all_to_all(result[None], 'shard', split_axis=1, concat_axis=0, tiled=...  16.9 us
    unnamed x1, other arithmetic  7.04 us
    unnamed x7, local copies, waits for them, and re-layouts  4.25 us
    dot_general x3, matrix products, transposed_product(): lax.dot_general(first_matrix, second_matrix, (((0,), (0,)), ((), ())), pr...  2.53 us
    dot_general x1, matrix products, polish(): jnp.dot(combined, quintic(current), preferred_element_type=jnp.float32)  2.29 us
    reduce_sum x1, other arithmetic, polish(): factor = 1.0 / (jnp.sqrt(jnp.trace(total)) + EPSILON)  2.21 us
    convert_element_type x1, other arithmetic, blended(): (gradient.astype(jnp.float32) + MOMENTUM_RATE * buffer).astype(jnp.bfloat16)  1.98 us
  transfers between devices with their start and end apart: 2, of which 2 were waited for; matrix products, arithmetic and copies ran while one was open for 0% of the time, Pallas kernels for 0%

commit v1 on v0

v1 whole, which is shorter than its diff:
```python
import functools
import math

import jax
import jax.numpy as jnp
from jax import lax
from jax.experimental import pallas as pl
from jax.experimental.pallas import tpu as pltpu
from jax.sharding import PartitionSpec as P

MOMENTUM_RATE = 0.95
COEF_A = 3.4445
COEF_B = -4.775
COEF_C = 2.0315
EPSILON = 1e-07
MESH = pl.DeviceIdType.MESH
BLOCK = 128
BF16 = jnp.bfloat16
F32 = jnp.float32


def blended(gradient, moment):
    buffer = MOMENTUM_RATE * moment.astype(F32) + gradient.astype(F32)
    return (gradient.astype(F32) + MOMENTUM_RATE * buffer).astype(BF16)


def product(first, second):
    return jnp.dot(first, second, preferred_element_type=F32)


def transposed_product(first, second):
    return lax.dot_general(first, second, (((0,), (0,)), ((), ())), preferred_element_type=F32)


def quintic(current, square):
    rows, columns = square.shape
    on_diagonal = lax.broadcasted_iota(jnp.int32, (rows, columns), 0) == lax.broadcasted_iota(
        jnp.int32, (rows, columns), 1
    )
    return jnp.where(on_diagonal, COEF_A, 0.0) + COEF_B * current.astype(F32) + COEF_C * square


def each(count, body):
    if count == 1:
        body(0)
    else:
        pl.loop(0, count)(body)


def kernel(
    shards,
    full_rows,
    gate_grad,
    gate_moment,
    down_grad,
    down_moment,
    out,
    inputs,
    blend,
    total,
    near_send,
    near_recv,
    far_send,
    far_recv,
    scaled_ref,
    combined_ref,
    other_ref,
    polished,
    input_sem,
    near_sems,
    far_sems,
    polished_sems,
):
    _, experts, rows, width = inputs.shape[1:]
    stages = shards.bit_length() - 2
    blocks = width // BLOCK
    me = lax.axis_index("shard")
    core = lax.rem(me, 2)
    near = me + 1 - 2 * core
    gate_slot, down_slot = 1 - core, core

    def far(stage):
        bit = lax.rem(me // (2 << stage), 2)
        return me + (1 - 2 * bit) * (2 << stage)

    loads = []
    for slot, pair in ((gate_slot, (gate_grad, gate_moment)), (down_slot, (down_grad, down_moment))):
        for member, source in enumerate(pair):
            loads.append(
                pltpu.make_async_copy(source, inputs.at[slot, member], input_sem.at[slot, member])
            )
    for load in loads:
        load.start()

    barrier = pltpu.get_barrier_semaphore()
    for peer in [near] + [far(stage) for stage in range(stages)]:
        pl.semaphore_signal(barrier, inc=1, device_id={"shard": peer}, device_id_type=MESH)

    def wait_loads(slot):
        for member in range(2):
            pltpu.make_async_copy(
                gate_grad, inputs.at[slot, member], input_sem.at[slot, member]
            ).wait()

    def upper(block):
        return pl.ds(block * BLOCK, BLOCK), pl.ds(block * BLOCK, width - block * BLOCK)

    def near_copy(expert, block):
        row, column = upper(block)
        return pltpu.make_async_remote_copy(
            src_ref=near_send.at[expert, row, column],
            dst_ref=near_recv.at[expert, row, column],
            send_sem=near_sems.at[0, expert, block],
            recv_sem=near_sems.at[1, expert, block],
            device_id={"shard": near},
            device_id_type=MESH,
        )

    def far_copy(stage, expert, block):
        row, column = upper(block)
        return pltpu.make_async_remote_copy(
            src_ref=far_send.at[expert, row, column],
            dst_ref=far_recv.at[stage, expert, row, column],
            send_sem=far_sems.at[0, stage, expert, block],
            recv_sem=far_sems.at[1, stage, expert, block],
            device_id={"shard": far(stage)},
            device_id_type=MESH,
        )

    def polished_copy(expert, block):
        row = pl.ds(block * BLOCK, BLOCK)
        return pltpu.make_async_remote_copy(
            src_ref=polished.at[1, expert, row],
            dst_ref=polished.at[0, expert, row],
            send_sem=polished_sems.at[0, expert, block],
            recv_sem=polished_sems.at[1, expert, block],
            device_id={"shard": near},
            device_id_type=MESH,
        )

    def blend_slot(slot, expert):
        blend[slot, expert] = blended(inputs[slot, 0, expert], inputs[slot, 1, expert])

    def gram(slot, expert, block):
        row, column = upper(block)
        return transposed_product(blend[slot, expert, :, row], blend[slot, expert, :, column])

    wait_loads(0)
    each(experts, lambda expert: blend_slot(0, expert))
    pl.semaphore_wait(barrier, 1 + stages)

    def send_other(expert):
        for block in range(blocks):
            row, column = upper(block)
            near_send[expert, row, column] = gram(0, expert, block).astype(BF16)
            near_copy(expert, block).start()

    each(experts, send_other)
    wait_loads(1)
    each(experts, lambda expert: blend_slot(1, expert))

    def own_total(expert):
        for block in range(blocks):
            row, column = upper(block)
            total[expert, row, column] = gram(1, expert, block)

    each(experts, own_total)

    def gather_near(expert):
        for block in range(blocks):
            row, column = upper(block)
            near_copy(expert, block).wait_recv()
            held = total[expert, row, column] + near_recv[expert, row, column].astype(F32)
            total[expert, row, column] = held
            if stages:
                far_send[expert, row, column] = held.astype(BF16)
                far_copy(0, expert, block).start()

    each(experts, gather_near)

    for stage in range(stages):
        if stage:

            def send_far(expert, stage=stage):
                for block in range(blocks):
                    row, column = upper(block)
                    far_copy(stage - 1, expert, block).wait_send()
                    far_send[expert, row, column] = total[expert, row, column].astype(BF16)
                    far_copy(stage, expert, block).start()

            each(experts, send_far)

        def gather_far(expert, stage=stage):
            for block in range(blocks):
                row, column = upper(block)
                far_copy(stage, expert, block).wait_recv()
                total[expert, row, column] = total[expert, row, column] + far_recv[
                    stage, expert, row, column
                ].astype(F32)

        each(experts, gather_far)

    def polish(expert):
        on_diagonal = lax.broadcasted_iota(jnp.int32, (BLOCK, BLOCK), 0) == lax.broadcasted_iota(
            jnp.int32, (BLOCK, BLOCK), 1
        )
        diagonal = jnp.zeros((BLOCK, BLOCK), F32)
        for block in range(blocks):
            row = pl.ds(block * BLOCK, BLOCK)
            diagonal = diagonal + jnp.where(on_diagonal, total[expert, row, row], 0.0)
        trace = jnp.sum(diagonal, axis=(0, 1), keepdims=True)
        factor = 1.0 / (jnp.sqrt(trace) + EPSILON)
        for block in range(blocks):
            row, column = upper(block)
            strip = (total[expert, row, column] * (factor * factor)).astype(BF16)
            scaled_ref[row, column] = strip
            for later in range(block + 1, blocks):
                start = (later - block) * BLOCK
                scaled_ref[pl.ds(later * BLOCK, BLOCK), row] = strip[:, start : start + BLOCK].T
        scaled = scaled_ref[...]
        combined_ref[...] = quintic(scaled, product(scaled, scaled)).astype(BF16)
        combined = combined_ref[...]
        other_ref[...] = product(scaled, combined).astype(BF16)
        scaled_ref[...] = product(combined, other_ref[...]).astype(BF16)
        current = scaled_ref[...]
        other_ref[...] = quintic(current, product(current, current)).astype(BF16)
        gain = math.sqrt(full_rows) * factor
        for block in range(blocks):
            row = pl.ds(block * BLOCK, BLOCK)
            polished[1, expert, row] = (product(combined_ref[row], other_ref[...]) * gain).astype(BF16)
            polished_copy(expert, block).start()

    each(experts, polish)

    def own_update(expert):
        out[core, expert] = product(blend[1, expert], polished[1, expert]).astype(BF16)

    each(experts, own_update)

    def other_update(expert):
        for block in range(blocks):
            polished_copy(expert, block).wait_recv()
        out[1 - core, expert] = product(blend[0, expert], polished[0, expert]).astype(BF16)

    each(experts, other_update)

    def drain(expert):
        for block in range(blocks):
            near_copy(expert, block).wait_send()
            if stages:
                far_copy(stages - 1, expert, block).wait_send()
            polished_copy(expert, block).wait_send()

    each(experts, drain)


def updates(shards, gate_grad, gate_moment, down_grad, down_moment):
    experts, rows, width = gate_grad.shape
    stages = max(shards.bit_length() - 2, 1)
    blocks = width // BLOCK
    out = pl.pallas_call(
        functools.partial(kernel, shards, rows * shards),
        out_shape=jax.ShapeDtypeStruct((2, experts, rows, width), BF16),
        in_specs=[pl.BlockSpec(memory_space=pl.ANY)] * 4,
        out_specs=pl.BlockSpec(memory_space=pltpu.VMEM),
        scratch_shapes=[
            pltpu.VMEM((2, 2, experts, rows, width), BF16),
            pltpu.VMEM((2, experts, rows, width), BF16),
            pltpu.VMEM((experts, width, width), F32),
            pltpu.VMEM((experts, width, width), BF16),
            pltpu.VMEM((experts, width, width), BF16),
            pltpu.VMEM((experts, width, width), BF16),
            pltpu.VMEM((stages, experts, width, width), BF16),
            pltpu.VMEM((width, width), BF16),
            pltpu.VMEM((width, width), BF16),
            pltpu.VMEM((width, width), BF16),
            pltpu.VMEM((2, experts, width, width), BF16),
            pltpu.SemaphoreType.DMA((2, 2)),
            pltpu.SemaphoreType.DMA((2, experts, blocks)),
            pltpu.SemaphoreType.DMA((2, stages, experts, blocks)),
            pltpu.SemaphoreType.DMA((2, experts, blocks)),
        ],
        compiler_params=pltpu.CompilerParams(collective_id=0, has_side_effects=True),
    )(gate_grad, gate_moment, down_grad, down_moment)
    return out[0], out[1]


def solution(mesh):
    placed = P("layer", "shard", None)
    return jax.shard_map(
        functools.partial(updates, mesh.shape["shard"]),
        mesh=mesh,
        in_specs=(placed,) * 4,
        out_specs=(placed,) * 2,
        check_vma=False,
    )
```

time: 64.3 us -> 22.3 us (0.35)
  the two profiles are of different devices: /device:TPU:0 before, /device:TPU:1 now
where the time goes in v1:
time: 22.3 us; the launch traced here: 22.1 us
  Pallas kernels  19.2 us (86%)
  local copies, waits for them, and re-layouts  2.23 us (10%)
  between operations  0.64 us (3%)
    pallas_call x1, Pallas kernels, updates(): pl.pallas_call(functools.partial(kernel, shards, rows * shards), out_shap...  19.2 us
    squeeze x1, local copies, waits for them, and re-layouts, updates(): return (out[0], out[1])  2.23 us

profile of v1, /device:TPU:1, one launch (start us, length us, event | category | flops | bytes accessed | tf_op | source)
XLA Modules:
  0.0 22.1 jit_solution(17139538810799041619)
XLA Ops:
  0.6 19.2 %shard_map.59 = bf16[2,1,512,512]{3,2,1,0:T(8,128)(2,1)} custom-call(bf16[1,512,512]{2,1,0:T(8,128)(2,1)} %gate_grad.1, bf16[1,512,512]{2,1,0:T(8,128)(2,1)} %gate_moment.1, bf16[1,512,512]{2,1,0:T(8,128)(2,1)} %down_grad.1, bf16[1,512,512]{2,1,0:T(8,128)(2,1)} %down_moment.1), custom_call_target="tpu_custom_call" | custom-call | tf_op jit(solution)/shard_map/pallas_call | solution.py:261
  19.8 2.2 %slice_bitcast_fusion = (bf16[1,512,512]{2,1,0:T(8,128)(2,1)}, bf16[1,512,512]{2,1,0:T(8,128)(2,1)}) fusion(bf16[2,1,512,512]{3,2,1,0:T(8,128)(2,1)} %shard_map.59), kind=kLoop, calls=%fused_computation | loop fusion | bytes 2097152 | tf_op jit(solution)/shard_map/squeeze | solution.py:285

commit v2 on v1

v2 whole, which is shorter than its diff:
```python
import functools
import math

import jax
import jax.numpy as jnp
from jax import lax
from jax.experimental import pallas as pl
from jax.experimental.pallas import tpu as pltpu
from jax.sharding import PartitionSpec as P

MOMENTUM_RATE = 0.95
COEF_A = 3.4445
COEF_B = -4.775
COEF_C = 2.0315
EPSILON = 1e-07
MESH = pl.DeviceIdType.MESH
BLOCK = 128
EXTRA = 16
BF16 = jnp.bfloat16
F32 = jnp.float32


def blended(gradient, moment):
    buffer = MOMENTUM_RATE * moment.astype(F32) + gradient.astype(F32)
    return (gradient.astype(F32) + MOMENTUM_RATE * buffer).astype(BF16)


def product(first, second):
    return jnp.dot(first, second, preferred_element_type=F32)


def transposed_product(first, second):
    return lax.dot_general(first, second, (((0,), (0,)), ((), ())), preferred_element_type=F32)


def iotas(size):
    return tuple(lax.broadcasted_iota(jnp.int32, (size, size), axis) for axis in range(2))


def quintic(current, square):
    row_at, column_at = iotas(square.shape[0])
    return jnp.where(row_at == column_at, COEF_A, 0.0) + COEF_B * current.astype(F32) + COEF_C * square


def each(count, body):
    if count == 1:
        body(0)
    else:
        pl.loop(0, count)(body)


def kernel(
    shards,
    full_rows,
    gate_grad,
    gate_moment,
    down_grad,
    down_moment,
    out,
    inputs,
    blend,
    total,
    first_ref,
    near_send,
    near_recv,
    far_send,
    far_recv,
    scaled_ref,
    combined_ref,
    other_ref,
    polished,
    input_sem,
    near_sems,
    far_sems,
    polished_sems,
):
    _, experts, rows, width = inputs.shape[1:]
    stages = shards.bit_length() - 2
    blocks, half = width // BLOCK, width // 2
    me = lax.axis_index("shard")
    core = lax.rem(me, 2)
    near = me + 1 - 2 * core

    def far(stage):
        bit = lax.rem(me // (2 << stage), 2)
        return me + (1 - 2 * bit) * (2 << stage)

    def load(slot, pair):
        for member, source in enumerate(pair):
            pltpu.make_async_copy(source, inputs.at[slot, member], input_sem.at[slot, member]).start()

    @pl.when(core == 0)
    def _():
        load(0, (down_grad, down_moment))
        load(1, (gate_grad, gate_moment))

    @pl.when(core == 1)
    def _():
        load(0, (gate_grad, gate_moment))
        load(1, (down_grad, down_moment))

    barrier = pltpu.get_barrier_semaphore()
    for peer in [near] + [far(stage) for stage in range(stages)]:
        pl.semaphore_signal(barrier, inc=1, device_id={"shard": peer}, device_id_type=MESH)

    def wait_loads(slot):
        for member in range(2):
            pltpu.make_async_copy(
                gate_grad, inputs.at[slot, member], input_sem.at[slot, member]
            ).wait()

    def part(block):
        return pl.ds(block * BLOCK, BLOCK + (EXTRA if block == blocks - 1 else 0))

    def near_copy(expert, block):
        row = part(block)
        return pltpu.make_async_remote_copy(
            src_ref=near_send.at[expert, row],
            dst_ref=near_recv.at[expert, row],
            send_sem=near_sems.at[0, expert, block],
            recv_sem=near_sems.at[1, expert, block],
            device_id={"shard": near},
            device_id_type=MESH,
        )

    def far_copy(stage, expert, block):
        row = part(block)
        return pltpu.make_async_remote_copy(
            src_ref=far_send.at[expert, row],
            dst_ref=far_recv.at[stage, expert, row],
            send_sem=far_sems.at[0, stage, expert, block],
            recv_sem=far_sems.at[1, stage, expert, block],
            device_id={"shard": far(stage)},
            device_id_type=MESH,
        )

    def polished_copy(expert, block):
        row = pl.ds(block * BLOCK, BLOCK)
        return pltpu.make_async_remote_copy(
            src_ref=polished.at[1, expert, row],
            dst_ref=polished.at[0, expert, row],
            send_sem=polished_sems.at[0, expert, block],
            recv_sem=polished_sems.at[1, expert, block],
            device_id={"shard": near},
            device_id_type=MESH,
        )

    def blend_slot(slot, expert):
        blend[slot, expert] = blended(inputs[slot, 0, expert], inputs[slot, 1, expert])

    def packed_gram(slot, expert, target, ready):
        matrix = blend[slot, expert]
        for block in range(blocks // 2):
            row = pl.ds(block * BLOCK, BLOCK)
            strip = transposed_product(matrix[:, block * BLOCK : (block + 1) * BLOCK], matrix)
            target[expert, row] = strip[:, half:].astype(target.dtype)
            ready(expert, block)
            first_ref[row] = strip[:, :half]
        last = transposed_product(matrix[:, half:], matrix[:, half:])
        row_at, column_at = iotas(half)
        target[expert, pl.ds(half, half)] = jnp.where(row_at <= column_at, first_ref[...], last).astype(
            target.dtype
        )
        diagonal = jnp.sum(jnp.where(row_at == column_at, last, 0.0), axis=0, keepdims=True)
        target[expert, pl.ds(width, EXTRA)] = jnp.broadcast_to(diagonal, (EXTRA, half)).astype(
            target.dtype
        )
        for block in range(blocks // 2, blocks):
            ready(expert, block)

    wait_loads(0)
    each(experts, lambda expert: blend_slot(0, expert))
    pl.semaphore_wait(barrier, 1 + stages)
    each(
        experts,
        lambda expert: packed_gram(
            0, expert, near_send, lambda at, block: near_copy(at, block).start()
        ),
    )
    wait_loads(1)
    each(experts, lambda expert: blend_slot(1, expert))
    each(experts, lambda expert: packed_gram(1, expert, total, lambda at, block: None))

    def gather_near(expert):
        for block in range(blocks):
            row = part(block)
            near_copy(expert, block).wait_recv()
            held = total[expert, row] + near_recv[expert, row].astype(F32)
            total[expert, row] = held
            if stages:
                far_send[expert, row] = held.astype(BF16)
                far_copy(0, expert, block).start()

    each(experts, gather_near)

    for stage in range(stages):
        if stage:

            def send_far(expert, stage=stage):
                for block in range(blocks):
                    row = part(block)
                    far_copy(stage - 1, expert, block).wait_send()
                    far_send[expert, row] = total[expert, row].astype(BF16)
                    far_copy(stage, expert, block).start()

            each(experts, send_far)

        def gather_far(expert, stage=stage):
            for block in range(blocks):
                row = part(block)
                far_copy(stage, expert, block).wait_recv()
                total[expert, row] = total[expert, row] + far_recv[stage, expert, row].astype(F32)

        each(experts, gather_far)

    def polish(expert):
        row_at, column_at = iotas(half)
        packed = total[expert, pl.ds(half, half)]
        diagonal = total[expert, pl.ds(width, 1)]
        kept = jnp.where(row_at == column_at, packed, 0.0)
        trace = jnp.sum(jnp.sum(kept, axis=0, keepdims=True) + diagonal, axis=1, keepdims=True)
        factor = 1.0 / (jnp.sqrt(trace) + EPSILON)
        square = factor * factor
        upper, lower = pl.ds(0, half), pl.ds(half, half)
        side = (total[expert, upper] * square).astype(BF16)
        scaled_ref[upper, lower] = side
        scaled_ref[lower, upper] = side.T
        packed = packed * square
        flipped = packed.T
        scaled_ref[upper, upper] = jnp.where(row_at <= column_at, packed, flipped).astype(BF16)
        scaled_ref[lower, lower] = jnp.where(
            row_at == column_at,
            diagonal * square,
            jnp.where(row_at > column_at, packed, flipped),
        ).astype(BF16)
        scaled = scaled_ref[...]
        combined_ref[...] = quintic(scaled, product(scaled, scaled)).astype(BF16)
        combined = combined_ref[...]
        other_ref[...] = product(scaled, combined).astype(BF16)
        scaled_ref[...] = product(combined, other_ref[...]).astype(BF16)
        current = scaled_ref[...]
        other_ref[...] = quintic(current, product(current, current)).astype(BF16)
        gain = math.sqrt(full_rows) * factor
        for block in range(blocks):
            row = pl.ds(block * BLOCK, BLOCK)
            polished[1, expert, row] = (product(combined_ref[row], other_ref[...]) * gain).astype(BF16)
            polished_copy(expert, block).start()

    each(experts, polish)

    def own_update(expert):
        out[core, expert] = product(blend[1, expert], polished[1, expert]).astype(BF16)

    each(experts, own_update)

    def other_update(expert):
        for block in range(blocks):
            polished_copy(expert, block).wait_recv()
        out[1 - core, expert] = product(blend[0, expert], polished[0, expert]).astype(BF16)

    each(experts, other_update)

    def drain(expert):
        for block in range(blocks):
            near_copy(expert, block).wait_send()
            if stages:
                far_copy(stages - 1, expert, block).wait_send()
            polished_copy(expert, block).wait_send()

    each(experts, drain)


def updates(shards, gate_grad, gate_moment, down_grad, down_moment):
    experts, rows, width = gate_grad.shape
    stages = max(shards.bit_length() - 2, 1)
    blocks = width // BLOCK
    packed = (width + EXTRA, width // 2)
    limit = experts * (24 * rows * width + (16 + 2 * stages) * width * width) + (16 << 20)
    out = pl.pallas_call(
        functools.partial(kernel, shards, rows * shards),
        out_shape=pltpu.VMEM((2, experts, rows, width), BF16),
        in_specs=[pl.BlockSpec(memory_space=pltpu.HBM)] * 4,
        out_specs=pl.BlockSpec(memory_space=pltpu.VMEM),
        scratch_shapes=[
            pltpu.VMEM((2, 2, experts, rows, width), BF16),
            pltpu.VMEM((2, experts, rows, width), BF16),
            pltpu.VMEM((experts, *packed), F32),
            pltpu.VMEM((width // 2, width // 2), F32),
            pltpu.VMEM((experts, *packed), BF16),
            pltpu.VMEM((experts, *packed), BF16),
            pltpu.VMEM((experts, *packed), BF16),
            pltpu.VMEM((stages, experts, *packed), BF16),
            pltpu.VMEM((width, width), BF16),
            pltpu.VMEM((width, width), BF16),
            pltpu.VMEM((width, width), BF16),
            pltpu.VMEM((2, experts, width, width), BF16),
            pltpu.SemaphoreType.DMA((2, 2)),
            pltpu.SemaphoreType.DMA((2, experts, blocks)),
            pltpu.SemaphoreType.DMA((2, stages, experts, blocks)),
            pltpu.SemaphoreType.DMA((2, experts, blocks)),
        ],
        compiler_params=pltpu.CompilerParams(collective_id=0, has_side_effects=True, vmem_limit_bytes=min(limit, 56 << 20)
        ),
    )(
        *(
            pltpu.with_memory_space_constraint(source, pltpu.HBM)
            for source in (gate_grad, gate_moment, down_grad, down_moment)
        )
    )
    return out[0], out[1]


def solution(mesh):
    placed = P("layer", "shard", None)
    return jax.shard_map(
        functools.partial(updates, mesh.shape["shard"]),
        mesh=mesh,
        in_specs=(placed,) * 4,
        out_specs=(placed,) * 2,
        check_vma=False,
    )
```

time: 22.3 us -> 18.6 us (0.83)
  the two profiles are of different devices: /device:TPU:1 before, /device:TPU:0 now
where the time goes in v2:
time: 18.6 us; the launch traced here: 18.5 us
  Pallas kernels  16.8 us (90%)
  local copies, waits for them, and re-layouts  1.03 us (6%)
  between operations  0.64 us (3%)
    pallas_call x1, Pallas kernels, updates(): pl.pallas_call(functools.partial(kernel, shards, rows * shards), out_shap...  16.8 us
    squeeze x1, local copies, waits for them, and re-layouts, updates(): return (out[0], out[1])  1.03 us

profile of v2, /device:TPU:0, one launch (start us, length us, event | category | flops | bytes accessed | tf_op | source)
XLA Modules:
  0.0 18.5 jit_solution(5832936281539579872)
XLA Ops:
  0.6 16.8 %shard_map.59 = bf16[2,1,512,512]{3,2,1,0:T(8,128)(2,1)S(1)} custom-call(bf16[1,512,512]{2,1,0:T(8,128)(2,1)} %gate_grad.1, bf16[1,512,512]{2,1,0:T(8,128)(2,1)} %gate_moment.1, bf16[1,512,512]{2,1,0:T(8,128)(2,1)} %down_grad.1, bf16[1,512,512]{2,1,0:T(8,128)(2,1)} %down_moment.1), custom_call_target="tpu_custom_call" | custom-call | tf_op jit(solution)/shard_map/pallas_call | solution.py:279
  17.4 1.0 %slice_bitcast_fusion = (bf16[1,512,512]{2,1,0:T(8,128)(2,1)}, bf16[1,512,512]{2,1,0:T(8,128)(2,1)}) fusion(bf16[2,1,512,512]{3,2,1,0:T(8,128)(2,1)S(1)} %shard_map.59), kind=kLoop, calls=%fused_computation | loop fusion | bytes 2097152 | tf_op jit(solution)/shard_map/squeeze | solution.py:310

commit v3 on v2

v3 whole, which is shorter than its diff:
```python
import functools
import math

import jax
import jax.numpy as jnp
from jax import lax
from jax.experimental import pallas as pl
from jax.experimental.pallas import tpu as pltpu
from jax.sharding import PartitionSpec as P

MOMENTUM_RATE = 0.95
COEF_A = 3.4445
COEF_B = -4.775
COEF_C = 2.0315
EPSILON = 1e-07
MESH = pl.DeviceIdType.MESH
BLOCK = 128
EXTRA = 16
BF16 = jnp.bfloat16
F32 = jnp.float32


def blended(gradient, moment):
    buffer = MOMENTUM_RATE * moment.astype(F32) + gradient.astype(F32)
    return (gradient.astype(F32) + MOMENTUM_RATE * buffer).astype(BF16)


def product(first, second):
    return jnp.dot(first, second, preferred_element_type=F32)


def transposed_product(first, second):
    return lax.dot_general(first, second, (((0,), (0,)), ((), ())), preferred_element_type=F32)


def iotas(size):
    return tuple(lax.broadcasted_iota(jnp.int32, (size, size), axis) for axis in range(2))


def quintic(current, square, start):
    row_at, column_at = (lax.broadcasted_iota(jnp.int32, square.shape, axis) for axis in range(2))
    return jnp.where(row_at + start == column_at, COEF_A, 0.0) + COEF_B * current.astype(F32) + COEF_C * square


def each(count, body):
    if count == 1:
        body(0)
    else:
        pl.loop(0, count)(body)


def kernel(
    shards,
    full_rows,
    gate_grad,
    gate_moment,
    down_grad,
    down_moment,
    own_out,
    other_half,
    other_second,
    inputs,
    blend,
    total,
    near_send,
    near_recv,
    far_send,
    far_recv,
    scaled_ref,
    first,
    first_other,
    second,
    current_ref,
    input_sem,
    near_sems,
    far_sems,
    polished_sems,
):
    _, experts, rows, width = inputs.shape[1:]
    stages = shards.bit_length() - 2
    blocks, strips, half = width // BLOCK, width // BLOCK // 2, width // 2
    me = lax.axis_index("shard")
    core = lax.rem(me, 2)
    near = me + 1 - 2 * core

    def far(stage):
        bit = lax.rem(me // (2 << stage), 2)
        return me + (1 - 2 * bit) * (2 << stage)

    barrier = pltpu.get_barrier_semaphore()
    for peer in [far(stage) for stage in range(stages)] + [near]:
        pl.semaphore_signal(barrier, inc=1, device_id={"shard": peer}, device_id_type=MESH)

    def load(slot, pair):
        for member, source in enumerate(pair):
            pltpu.make_async_copy(source, inputs.at[slot, member], input_sem.at[slot, member]).start()

    @pl.when(core == 0)
    def _():
        load(0, (down_grad, down_moment))
        load(1, (gate_grad, gate_moment))

    @pl.when(core == 1)
    def _():
        load(0, (gate_grad, gate_moment))
        load(1, (down_grad, down_moment))

    def wait_loads(slot):
        for member in range(2):
            pltpu.make_async_copy(
                gate_grad, inputs.at[slot, member], input_sem.at[slot, member]
            ).wait()

    def part(block):
        if block < strips:
            return pl.ds(block * BLOCK, BLOCK + (EXTRA if block == strips - 1 else 0))
        return pl.ds(EXTRA + block * BLOCK, BLOCK)

    def near_copy(expert, block):
        row = part(block)
        return pltpu.make_async_remote_copy(
            src_ref=near_send.at[expert, row],
            dst_ref=near_recv.at[expert, row],
            send_sem=near_sems.at[0, expert, block],
            recv_sem=near_sems.at[1, expert, block],
            device_id={"shard": near},
            device_id_type=MESH,
        )

    def far_copy(stage, expert, block):
        row = part(block)
        return pltpu.make_async_remote_copy(
            src_ref=far_send.at[expert, row],
            dst_ref=far_recv.at[stage, expert, row],
            send_sem=far_sems.at[0, stage, expert, block],
            recv_sem=far_sems.at[1, stage, expert, block],
            device_id={"shard": far(stage)},
            device_id_type=MESH,
        )

    def first_copy(expert):
        return pltpu.make_async_remote_copy(
            src_ref=first.at[expert],
            dst_ref=first_other.at[expert],
            send_sem=polished_sems.at[0, expert, blocks],
            recv_sem=polished_sems.at[1, expert, blocks],
            device_id={"shard": near},
            device_id_type=MESH,
        )

    def second_copy(expert, block):
        row = pl.ds(block * BLOCK, BLOCK)
        return pltpu.make_async_remote_copy(
            src_ref=second.at[expert, row],
            dst_ref=other_second.at[expert, row],
            send_sem=polished_sems.at[0, expert, block],
            recv_sem=polished_sems.at[1, expert, block],
            device_id={"shard": near},
            device_id_type=MESH,
        )

    def blend_slot(slot, expert):
        blend[slot, expert] = blended(inputs[slot, 0, expert], inputs[slot, 1, expert])

    def packed_gram(slot, expert, target, ready):
        matrix = blend[slot, expert]
        diagonal = jnp.zeros((1, half), F32)
        row_at, column_at = (at[:BLOCK] for at in iotas(half))
        for block in range(strips):
            start = block * BLOCK
            strip = transposed_product(matrix[:, start : start + BLOCK], matrix)
            last = transposed_product(matrix[:, half + start : half + start + BLOCK], matrix[:, half:])
            target[expert, part(strips + block)] = strip[:, half:].astype(target.dtype)
            target[expert, pl.ds(start, BLOCK)] = jnp.where(
                row_at + start <= column_at, strip[:, :half], last
            ).astype(target.dtype)
            diagonal = diagonal + jnp.sum(
                jnp.where(row_at + start == column_at, last, 0.0), axis=0, keepdims=True
            )
            if block == strips - 1:
                target[expert, pl.ds(half, EXTRA)] = jnp.broadcast_to(diagonal, (EXTRA, half)).astype(
                    target.dtype
                )
            ready(expert, block)
        for block in range(strips, blocks):
            ready(expert, block)

    def enter():
        pl.semaphore_wait(barrier, 1 + stages)

    def send_near(expert, block):
        if experts == 1 and block == 0:
            enter()
        near_copy(expert, block).start()

    def gather_near(expert, block):
        row = part(block)
        near_copy(expert, block).wait_recv()
        held = total[expert, row] + near_recv[expert, row].astype(F32)
        total[expert, row] = held
        if stages:
            far_send[expert, row] = held.astype(BF16)
            far_copy(0, expert, block).start()

    wait_loads(0)
    each(experts, lambda expert: blend_slot(0, expert))
    if experts > 1:
        enter()
    each(experts, lambda expert: packed_gram(0, expert, near_send, send_near))
    wait_loads(1)
    each(experts, lambda expert: blend_slot(1, expert))
    each(experts, lambda expert: packed_gram(1, expert, total, gather_near))

    for stage in range(stages):
        if stage:

            def send_far(expert, stage=stage):
                for block in range(blocks):
                    row = part(block)
                    far_copy(stage - 1, expert, block).wait_send()
                    far_send[expert, row] = total[expert, row].astype(BF16)
                    far_copy(stage, expert, block).start()

            each(experts, send_far)

        def gather_far(expert, block, stage=stage):
            row = part(block)
            far_copy(stage, expert, block).wait_recv()
            held = total[expert, row] + far_recv[stage, expert, row].astype(F32)
            total[expert, row] = held

        def gather_strips(expert, gather_far=gather_far):
            for block in range(blocks):
                gather_far(expert, block)

        if stage < stages - 1:
            each(experts, gather_strips)

    def polish(expert):
        row_at, column_at = iotas(half)
        for block in range(strips if stages else 0):
            gather_far(expert, block)
        packed = total[expert, pl.ds(0, half)]
        diagonal = total[expert, pl.ds(half, 1)]
        kept = jnp.where(row_at == column_at, packed, 0.0)
        trace = jnp.sum(jnp.sum(kept, axis=0, keepdims=True) + diagonal, axis=1, keepdims=True)
        factor = 1.0 / (jnp.sqrt(trace) + EPSILON)
        square = factor * factor
        upper, lower = pl.ds(0, half), pl.ds(half, half)
        packed = packed * square
        flipped = packed.T
        scaled_ref[upper, upper] = jnp.where(row_at <= column_at, packed, flipped).astype(BF16)
        scaled_ref[lower, lower] = jnp.where(
            row_at == column_at,
            diagonal * square,
            jnp.where(row_at > column_at, packed, flipped),
        ).astype(BF16)
        for block in range(strips):
            if stages:
                gather_far(expert, strips + block)
            row = pl.ds(block * BLOCK, BLOCK)
            side = (total[expert, part(strips + block)] * square).astype(BF16)
            scaled_ref[row, lower] = side
            scaled_ref[lower, row] = side.T
        scaled = scaled_ref[...]
        first[expert] = quintic(scaled, product(scaled, scaled), 0).astype(BF16)
        first_copy(expert).start()
        current_ref[...] = product(scaled, first[expert]).astype(BF16)
        scaled_ref[...] = product(first[expert], current_ref[...]).astype(BF16)
        gain = math.sqrt(full_rows) * factor
        for block in range(blocks):
            row = pl.ds(block * BLOCK, BLOCK)
            current = scaled_ref[row]
            step = quintic(current, product(current, scaled_ref[...]), block * BLOCK)
            second[expert, row] = (step * gain).astype(BF16)
            second_copy(expert, block).start()

    each(experts, polish)

    def own_update(expert):
        halfway = product(blend[1, expert], first[expert]).astype(BF16)
        own_out[expert] = product(halfway, second[expert]).astype(BF16)

    each(experts, own_update)

    def other_update(expert):
        first_copy(expert).wait_recv()
        other_half[expert] = product(blend[0, expert], first_other[expert]).astype(BF16)

    each(experts, other_update)

    def drain(expert):
        first_copy(expert).wait_send()
        for block in range(blocks):
            second_copy(expert, block).wait_recv()
            second_copy(expert, block).wait_send()
            near_copy(expert, block).wait_send()
            if stages:
                far_copy(stages - 1, expert, block).wait_send()

    each(experts, drain)


def finish(own, other_half, other_second, gate, down, other, sems):
    experts, rows, _ = own.shape
    core = lax.rem(lax.axis_index("shard"), 2)
    pieces = sems.shape[0] - 1

    def copies(source, target, piece):
        row = pl.ds(0, rows) if piece == pieces else pl.ds(piece * (rows // pieces), rows // pieces)
        return pltpu.make_async_copy(source.at[:, row], target.at[:, row], sems.at[piece])

    def start(source, piece, low, high):
        pl.when(core == 0)(lambda: copies(source, low, piece).start())
        pl.when(core == 1)(lambda: copies(source, high, piece).start())

    start(own, pieces, gate, down)
    for piece in range(pieces):
        row = pl.ds(piece * (rows // pieces), rows // pieces)

        def update(expert, row=row):
            other[expert, row] = product(other_half[expert, row], other_second[expert]).astype(BF16)

        each(experts, update)
        start(other, piece, down, gate)
    for piece in range(pieces + 1):
        copies(other, gate, piece).wait()


def updates(shards, gate_grad, gate_moment, down_grad, down_moment):
    experts, rows, width = gate_grad.shape
    stages = max(shards.bit_length() - 2, 1)
    blocks = width // BLOCK
    packed = (width + EXTRA, width // 2)
    limit = experts * (24 * rows * width + (16 + 2 * stages) * width * width) + (16 << 20)
    own, other_half, other_second = pl.pallas_call(
        functools.partial(kernel, shards, rows * shards),
        out_shape=(
            pltpu.VMEM((experts, rows, width), BF16),
            pltpu.VMEM((experts, rows, width), BF16),
            pltpu.VMEM((experts, width, width), BF16),
        ),
        in_specs=[pl.BlockSpec(memory_space=pltpu.HBM)] * 4,
        out_specs=(pl.BlockSpec(memory_space=pltpu.VMEM),) * 3,
        scratch_shapes=[
            pltpu.VMEM((2, 2, experts, rows, width), BF16),
            pltpu.VMEM((2, experts, rows, width), BF16),
            pltpu.VMEM((experts, *packed), F32),
            pltpu.VMEM((experts, *packed), BF16),
            pltpu.VMEM((experts, *packed), BF16),
            pltpu.VMEM((experts, *packed), BF16),
            pltpu.VMEM((stages, experts, *packed), BF16),
            pltpu.VMEM((width, width), BF16),
            pltpu.VMEM((experts, width, width), BF16),
            pltpu.VMEM((experts, width, width), BF16),
            pltpu.VMEM((experts, width, width), BF16),
            pltpu.VMEM((width, width), BF16),
            pltpu.SemaphoreType.DMA((2, 2)),
            pltpu.SemaphoreType.DMA((2, experts, blocks)),
            pltpu.SemaphoreType.DMA((2, stages, experts, blocks)),
            pltpu.SemaphoreType.DMA((2, experts, blocks + 1)),
        ],
        compiler_params=pltpu.CompilerParams(collective_id=0, has_side_effects=True, vmem_limit_bytes=min(limit, 56 << 20)
        ),
    )(
        *(
            pltpu.with_memory_space_constraint(source, pltpu.HBM)
            for source in (gate_grad, gate_moment, down_grad, down_moment)
        )
    )
    result = jax.ShapeDtypeStruct((experts, rows, width), BF16)
    return pl.pallas_call(
        finish,
        out_shape=(result, result),
        in_specs=[pl.BlockSpec(memory_space=pltpu.VMEM)] * 3,
        out_specs=(pl.BlockSpec(memory_space=pl.ANY),) * 2,
        scratch_shapes=[
            pltpu.VMEM((experts, rows, width), BF16),
            pltpu.SemaphoreType.DMA((3,)),
        ],
        compiler_params=pltpu.CompilerParams(vmem_limit_bytes=8 << 20),
    )(own, other_half, other_second)


def solution(mesh):
    placed = P("layer", "shard", None)
    return jax.shard_map(
        functools.partial(updates, mesh.shape["shard"]),
        mesh=mesh,
        in_specs=(placed,) * 4,
        out_specs=(placed,) * 2,
        check_vma=False,
    )
```

time: 18.6 us -> 18.5 us (level)
  local copies, waits for them, and re-layouts: 1.03 us -> 0 us
  Pallas kernels: 16.8 us -> 17.7 us
    pallas_call x0 -> x1, Pallas kernels: none -> 1.2 us  [updates(): pl.pallas_call(finish, out_shape=(result, result), in_specs=[pl.BlockSpec...]
    squeeze x1 -> x0, local copies, waits for them, and re-layouts: 1.03 us -> none  [updates(): return (out[0], out[1])]
    pallas_call x1, Pallas kernels: 16.8 us -> 16.6 us  [updates(): pl.pallas_call(functools.partial(kernel, shards, rows * shards), out_shap...]
where the time goes in v3:
time: 18.5 us; the launch traced here: 18.4 us
  Pallas kernels  17.7 us (96%)
  between operations  0.64 us (3%)
    pallas_call x1, Pallas kernels, updates(): pl.pallas_call(functools.partial(kernel, shards, rows * shards), out_shap...  16.6 us
    pallas_call x1, Pallas kernels, updates(): pl.pallas_call(finish, out_shape=(result, result), in_specs=[pl.BlockSpec...  1.2 us

profile of v3, /device:TPU:0, one launch (start us, length us, event | category | flops | bytes accessed | tf_op | source)
XLA Modules:
  0.0 18.4 jit_solution(703596562424434971)
XLA Ops:
  0.6 16.6 %shard_map.59 = (bf16[1,512,512]{2,1,0:T(8,128)(2,1)S(1)}, bf16[1,512,512]{2,1,0:T(8,128)(2,1)S(1)}, bf16[1,512,512]{2,1,0:T(8,128)(2,1)S(1)}) custom-call(bf16[1,512,512]{2,1,0:T(8,128)(2,1)} %gate_grad.1, bf16[1,512,512]{2,1,0:T(8,128)(2,1)} %gate_moment.1, bf16[1,512,512]{2,1,0:T(8,128)(2,1)} %down_grad.1, bf16[1,512,512]{2,1,0:T(8,128)(2,1)} %down_moment.1), custom_call_target="tpu_custom_call" | custom-call | tf_op jit(solution)/shard_map/pallas_call | solution.py:336
  17.2 1.2 %shard_map.60 = (bf16[1,512,512]{2,1,0:T(8,128)(2,1)}, bf16[1,512,512]{2,1,0:T(8,128)(2,1)}) custom-call(bf16[1,512,512]{2,1,0:T(8,128)(2,1)S(1)} %get-tuple-element.5.own, bf16[1,512,512]{2,1,0:T(8,128)(2,1)S(1)} %get-tuple-element.6.other_half, bf16[1,512,512]{2,1,0:T(8,128)(2,1)S(1)} %get-tuple-element.7.other_second), custom_call_target="tpu_custom_call" | custom-call | tf_op jit(solution)/shard_map/pallas_call | solution.py:372
